TPU v7x, 32 devices: a whole 2x2x4 slice. The times are simulated.
32 devices in a mesh: occ: 8 (over y, x, core), vir: 4 (over z).
Axes of the slice: x: 2, y: 2, z: 4, core: 2. Of those that a mesh axis runs over, the one named last changes fastest.
Arguments:
- factors: bfloat16 [8, 1024, 2048], P('occ', 'vir'), may hold values from -0.047851562 to 0.047851562
- occupied_energy: float32 [8], replicated, may hold values from -1.5 to -0.5
- virtual_energy: float32 [1024], replicated, may hold values from 0.2 to 3
Outputs:
- dens_vv: float32 [1024, 1024], P(('occ', 'vir'))
- dens_oo: float32 [8, 8], replicated
All inputs are finite; a program needn't handle non-finite values.
Results may differ from a plain program's by a relative error of at most 0.0065.
Values may be sent and summed in bfloat16 or wider, within the bound.
No kernel may reach another device: no remote copies, remote signals or barrier semaphores. Data moves between devices by JAX's collectives and lax.ppermute only.
A program may use at most 64 MiB of HBM per device.

v0:
```python
import jax
import jax.numpy as jnp
from jax import lax
from jax.sharding import PartitionSpec as P


def from_behind(shard, axis, by):
    length = lax.axis_size(axis)
    return lax.ppermute(shard, axis, [(i, (i + by) % length) for i in range(length)])


def on_device(factors, occupied_energy, virtual_energy):
    orbitals = factors.shape[0]
    vblock = factors.shape[1]
    nvir_all = virtual_energy.shape[0]
    nbatch_all = occupied_energy.shape[0]
    occ_count = lax.axis_size("occ")
    vir_count = lax.axis_size("vir")
    partners = occ_count // 4
    occ_pos = lax.axis_index("occ")
    vir_pos = lax.axis_index("vir")
    highest = lax.Precision.HIGHEST
    whole = lax.all_gather(factors, "vir", axis=1, tiled=True)

    def tiles(block):
        return jnp.einsum(
            "sjyp,ixp->isjyx", block, whole, preferred_element_type=jnp.float32
        ).astype(jnp.bfloat16)

    stack = jnp.zeros((orbitals, partners, orbitals, vblock, nvir_all), jnp.bfloat16)
    stack = lax.dynamic_update_slice_in_dim(stack, tiles(factors[None]), 0, 1)

    def advance(position, carry):
        current, filled = carry
        current = from_behind(current, "occ", -1)
        filled = lax.dynamic_update_slice_in_dim(filled, tiles(current[None]), position, 1)
        return (current, filled)

    _, stack = lax.fori_loop(1, partners, advance, (factors, stack))
    sending = stack.reshape(orbitals, partners, orbitals, vblock, vir_count, nvir_all // vir_count)
    received = lax.all_to_all(sending, "vir", split_axis=4, concat_axis=4, tiled=True)
    coulomb = received.transpose(0, 1, 2, 5, 4, 3).reshape(
        orbitals, partners, orbitals, vblock, nvir_all
    )
    batch_ids = (occ_pos + jnp.arange(partners, dtype=jnp.int32)) % occ_count
    global_ids = (
        batch_ids[:, None] * orbitals + jnp.arange(orbitals, dtype=jnp.int32)[None, :]
    ).reshape(-1)
    onehot = (global_ids[:, None] == jnp.arange(nbatch_all, dtype=jnp.int32)[None, :]).astype(
        jnp.float32
    )
    partner_energy = jnp.dot(onehot, occupied_energy, precision=highest).reshape(partners, orbitals)
    own_energy = lax.dynamic_slice_in_dim(occupied_energy, occ_pos * orbitals, orbitals)
    local_vir = lax.dynamic_slice_in_dim(virtual_energy, vir_pos * vblock, vblock)
    denom = (
        own_energy[:, None, None, None, None]
        + partner_energy[None, :, :, None, None]
        - local_vir[:, None]
        - virtual_energy
    )
    amps = (coulomb.astype(jnp.float32) / denom).astype(jnp.bfloat16)
    tilde = ((2.0 * coulomb.astype(jnp.float32) - stack.astype(jnp.float32)) / denom).astype(
        jnp.bfloat16
    )
    flat_amps = amps.reshape(-1, nvir_all)
    flat_tilde = tilde.reshape(-1, nvir_all)
    partial_rows = lax.psum_scatter(
        lax.dot_general(
            flat_amps, flat_tilde, (((0,), (0,)), ((), ())), preferred_element_type=jnp.float32
        ).astype(jnp.bfloat16),
        "occ",
        scatter_dimension=0,
        tiled=True,
    ).astype(jnp.float32)
    dens_vv = lax.psum_scatter(partial_rows, "vir", scatter_dimension=0, tiled=True)
    amps_rows = amps.reshape(orbitals, partners * orbitals, -1)
    tilde_rows = tilde.reshape(orbitals, partners * orbitals, -1)
    gram = -lax.dot_general(
        amps_rows, tilde_rows, (((2,), (2,)), ((0,), (0,))), preferred_element_type=jnp.float32
    )
    gram_sum = jnp.sum(gram, axis=0)
    placed = jnp.dot(onehot.T, jnp.dot(gram_sum, onehot, precision=highest), precision=highest)
    dens_oo = lax.psum(placed, ("occ", "vir"))
    return (dens_vv, dens_oo)


def solution(mesh):
    return jax.shard_map(
        on_device,
        mesh=mesh,
        in_specs=(P("occ", "vir", None), P(), P()),
        out_specs=(P(("occ", "vir"), None), P()),
        check_vma=False,
    )
```

profile of v0, /device:TPU:0, one launch (start us, length us, event | category | flops | bytes accessed | tf_op | source)
XLA Modules:
  0.0 227.3 jit_solution(8085726508122237578)
XLA Ops:
  7.2 0.7 all-gather.2.cloned.1.call-update
  7.9 3.4 %collective-permute-start = (bf16[1,256,2048]{2,1,0:T(8,128)(2,1)}, bf16[1,256,2048]{2,1,0:T(8,128)(2,1)S(1)}, u32[]{:S(2)}, u32[]{:S(2)}) collective-permute-start(bf16[1,256,2048]{2,1,0:T(8,128)(2,1)} %param.3), channel_id=1, source_target_pairs={{0,28},{4,0},{8,4},{12,8},{16,12},{20,16},{24,20},{28,24},{1,29},{... | collective-permute-start | bytes 3145736 | tf_op jit(solution)/shard_map/while/body/eval_jaxpr/ppermute | solution.py:9
  11.3 81.7 %all-gather.2.cloned.1.call-done = bf16[1,1024,2048]{2,1,0:T(8,128)(2,1)} async-done(((bf16[1,256,2048]{2,1,0:T(8,128)(2,1)}), bf16[1,1024,2048]{2,1,0:T(8,128)(2,1)}) %all-gather.2.cloned.1.call-update) | async-done | bytes 4194320 | tf_op jit(solution)/shard_map/all_gather | solution.py:23
  93.0 3.9 %fusion.7 = bf16[1024,256]{1,0:T(8,128)(2,1)S(1)} fusion(bf16[1,1024,2048]{2,1,0:T(8,128)(2,1)} %all-gather.2.cloned.1.call-done, bf16[1,256,2048]{2,1,0:T(8,128)(2,1)} %param.3), kind=kOutput, calls=%fused_computation.11 | convolution fusion | flops 1074003968 | bytes 5767168 | tf_op jit(solution)/shard_map/sjyp,ixp->isjyx/dot_general | solution.py:26
  97.0 1.4 fusion.10
  98.4 0.1 pad_maximum_fusion
  98.5 1.3 copy.10
  99.8 3.5 %all-to-all-start = ((bf16[1,2,1,256,4,256]{5,3,2,1,0,4:T(8,128)(2,1)}), bf16[1,2,1,256,4,256]{5,3,2,1,0,4:T(8,128)(2,1)S(1)}, u32[]{:S(2)}, u32[]{:S(2)}) async-start(bf16[1,2,1,256,4,256]{5,3,2,1,0,4:T(8,128)(2,1)} %copy.10), calls=%async_computation | async-start | bytes 2097152 | tf_op jit(solution)/shard_map/all_to_all | solution.py:41
  103.3 0.0 reduce-scatter.3.cloned.1.call-start
  103.4 0.1 dynamic_slice.7
  103.5 0.6 dynamic_slice.6
  104.1 0.8 fusion.14
  104.9 0.1 broadcast_subtract_fusion
  105.0 24.2 %all-to-all-done = bf16[1,2,1,256,4,256]{5,3,2,1,0,4:T(8,128)(2,1)S(1)} async-done(((bf16[1,2,1,256,4,256]{5,3,2,1,0,4:T(8,128)(2,1)}), bf16[1,2,1,256,4,256]{5,3,2,1,0,4:T(8,128)(2,1)S(1)}, u32[]{:S(2)}, u32[]{:S(2)}) %all-to-all-start) | async-done | bytes 1048608 | tf_op jit(solution)/shard_map/all_to_all | solution.py:41
  129.2 1.9 fusion.5
  131.0 2.6 %bitcast_convert_fusion = bf16[1024,1024]{1,0:T(8,128)(2,1)} fusion(bf16[2,256,1024]{1,2,0:T(8,128)(2,1)S(1)} %bitcast.65, bf16[2,256,1024]{1,2,0:T(8,128)(2,1)S(1)} %bitcast.63), kind=kOutput, calls=%fused_computation | convolution fusion | flops 1074790400 | bytes 4194304 | tf_op jit(solution)/shard_map/dot_general | solution.py:68
  133.7 40.3 %reduce-scatter.3.cloned.1.call-done = bf16[128,1024]{1,0:T(8,128)(2,1)} async-done(((bf16[1024,1024]{1,0:T(8,128)(2,1)}), bf16[128,1024]{1,0:T(8,128)(2,1)}) %reduce-scatter.3.cloned.1.call-update) | async-done | bytes 262160 | tf_op jit(solution)/shard_map/reduce_scatter | solution.py:67
  174.0 1.8 convert_element_type.89
  175.8 1.1 copy.15
  176.9 1.1 copy.16
  178.1 3.0 %fusion.13 = f32[2,2]{1,0:T(2,128)S(1)} fusion(bf16[2,256,4,256]{3,0,2,1:T(2,128)(2,1)S(1)} %copy.15, bf16[2,256,4,256]{3,0,2,1:T(2,128)(2,1)S(1)} %copy.16), kind=kOutput, calls=%fused_computation.14 | convolution fusion | flops 2097156 | bytes 2097168 | tf_op jit(solution)/shard_map/dot_general | solution.py:78
  181.1 0.2 fusion.18
  181.3 0.3 fusion.17
  181.5 39.2 %psum.7 = f32[8,8]{1,0:T(8,128)} all-reduce(f32[8,8]{1,0:T(8,128)S(1)} %fusion.17), channel_id=1, replica_groups=mesh['occ'=8,'vir'=4] {'occ','vir'}, use_global_device_ids=true, to_apply=%region_2.3 | all-reduce | flops 64 | bytes 512 | tf_op jit(solution)/shard_map/psum | solution.py:83
  (18 shorter events, 0.2 us)
Async XLA Ops:
  7.2 85.9 %all-gather.2.cloned.1.call-start = ((), (), s32[]{:S(2)}) async-start(), calls=%async_computation.3 | async-start | bytes 5242880 | tf_op jit(solution)/shard_map/all_gather | solution.py:23
  7.9 89.1 %collective-permute-start = (bf16[1,256,2048]{2,1,0:T(8,128)(2,1)}, bf16[1,256,2048]{2,1,0:T(8,128)(2,1)S(1)}, u32[]{:S(2)}, u32[]{:S(2)}) collective-permute-start(bf16[1,256,2048]{2,1,0:T(8,128)(2,1)} %param.3), channel_id=1, source_target_pairs={{0,28},{4,0},{8,4},{12,8},{16,12},{20,16},{24,20},{28,24},{1,29},{... | collective-permute-start | bytes 3145736 | tf_op jit(solution)/shard_map/while/body/eval_jaxpr/ppermute | solution.py:9
  93.0 4.0 %copy-start.3 = (bf16[1,1024,2048]{2,1,0:T(8,128)(2,1)S(1)}, bf16[1,1024,2048]{2,1,0:T(8,128)(2,1)}, u32[]{:S(2)}) copy-start(bf16[1,1024,2048]{2,1,0:T(8,128)(2,1)} %all-gather.2.cloned.1.call-done) | copy-start | bytes 12582916
  97.0 1.4 copy-start
  98.4 1.4 copy-start.1
  98.5 4.9 %copy-start.2 = (f32[1024]{0:T(1024)S(1)}, f32[1024]{0:T(1024)}, u32[]{:S(2)}) copy-start(f32[1024]{0:T(1024)} %param.5) | copy-start | bytes 12292
  98.5 5.0 %copy-start.4 = (f32[8]{0:T(128)S(1)}, f32[8]{0:T(128)}, u32[]{:S(2)}) copy-start(f32[8]{0:T(128)} %param.4) | copy-start | bytes 100
  99.8 29.4 %all-to-all-start = ((bf16[1,2,1,256,4,256]{5,3,2,1,0,4:T(8,128)(2,1)}), bf16[1,2,1,256,4,256]{5,3,2,1,0,4:T(8,128)(2,1)S(1)}, u32[]{:S(2)}, u32[]{:S(2)}) async-start(bf16[1,2,1,256,4,256]{5,3,2,1,0,4:T(8,128)(2,1)} %copy.10), calls=%async_computation | async-start | bytes 2097152 | tf_op jit(solution)/shard_map/all_to_all | solution.py:41
  103.3 70.7 %reduce-scatter.3.cloned.1.call-start = ((), (), s32[]{:S(2)}) async-start(), calls=%async_computation.4 | async-start | bytes 2359296 | tf_op jit(solution)/shard_map/reduce_scatter | solution.py:67
  133.7 87.1 %reduce-scatter.5.cloned.1.call-start = ((), (), s32[]{:S(2)}) async-start(), calls=%async_computation.5 | async-start | bytes 655360 | tf_op jit(solution)/shard_map/reduce_scatter | solution.py:75
Sparse Core Ops, SparseCore 0:
  9.5 83.4 all-gather.1
  133.8 40.1 reduce-scatter.2
  176.9 21.8 reduce-scatter.4
where the time goes:
time: 228 us; the launch traced here: 227 us
  waiting for transfers between devices  147 us (64%)
  blocking collectives  39.2 us (17%)
  between operations  13.9 us (6%)
  matrix products  12.2 us (5%)
  starting transfers between devices  7.05 us (3%)
  local copies, waits for them, and re-layouts  4.21 us (2%)
  other arithmetic  3.84 us (2%)
    all_gather x1, waiting for transfers between devices, on_device(): whole = lax.all_gather(factors, 'vir', axis=1, tiled=True)  81.7 us
    reduce_scatter x1, waiting for transfers between devices, on_device(): lax.psum_scatter(lax.dot_general(flat_amps, flat_tilde, (((0,), (0,)), ((...  40.3 us
    psum x1, blocking collectives, on_device(): dens_oo = lax.psum(placed, ('occ', 'vir'))  39.2 us
    all_to_all x1, waiting for transfers between devices, on_device(): lax.all_to_all(sending, 'vir', split_axis=4, concat_axis=4, tiled=True)  24.2 us
    dot_general x2, matrix products, tiles(): jnp.einsum('sjyp,ixp->isjyx', block, whole, preferred_element_type=jnp.fl...  5.27 us
  transfers between devices with their start and end apart: 5, of which 3 were waited for; matrix products, arithmetic and copies ran while one was open for 5% of the time, Pallas kernels for 0%

commit v1 on v0

--- a/solution.py
+++ b/solution.py
@@ -80,7 +80,7 @@
     )
     gram_sum = jnp.sum(gram, axis=0)
     placed = jnp.dot(onehot.T, jnp.dot(gram_sum, onehot, precision=highest), precision=highest)
-    dens_oo = lax.psum(placed, ("occ", "vir"))
+    dens_oo = jnp.sum(lax.all_gather(placed, ("occ", "vir")), axis=0)
     return (dens_vv, dens_oo)
 
 

time: 228 us -> 257 us (1.13)
  blocking collectives: 39.2 us -> 68.1 us
    all_gather x0 -> x1, blocking collectives: none -> 68.1 us  [on_device(): dens_oo = jnp.sum(lax.all_gather(placed, ('occ', 'vir')), axis=0)]
    psum x1 -> x0, blocking collectives: 39.2 us -> none  [on_device(): dens_oo = lax.psum(placed, ('occ', 'vir'))]
where the time goes in v1:
time: 257 us
  waiting for transfers between devices  147 us (57%)
  blocking collectives  68.1 us (26%)
  between operations  13.9 us (5%)
  matrix products  12.2 us (5%)
  starting transfers between devices  7.05 us (3%)
  other arithmetic  4.47 us (2%)
  local copies, waits for them, and re-layouts  4.21 us (2%)
    all_gather x1, waiting for transfers between devices, on_device(): whole = lax.all_gather(factors, 'vir', axis=1, tiled=True)  81.7 us
    all_gather x1, blocking collectives, on_device(): dens_oo = jnp.sum(lax.all_gather(placed, ('occ', 'vir')), axis=0)  68.1 us
    reduce_scatter x1, waiting for transfers between devices, on_device(): lax.psum_scatter(lax.dot_general(flat_amps, flat_tilde, (((0,), (0,)), ((...  40.3 us
    all_to_all x1, waiting for transfers between devices, on_device(): lax.all_to_all(sending, 'vir', split_axis=4, concat_axis=4, tiled=True)  24.2 us
    dot_general x2, matrix products, tiles(): jnp.einsum('sjyp,ixp->isjyx', block, whole, preferred_element_type=jnp.fl...  5.27 us
  transfers between devices with their start and end apart: 5, of which 3 were waited for; matrix products, arithmetic and copies ran while one was open for 5% of the time, Pallas kernels for 0%

profile of v1, /device:TPU:0, one launch (start us, length us, event | category | flops | bytes accessed | tf_op | source)
XLA Modules:
  0.0 256.8 jit_solution(14425997450792401202)
XLA Ops:
  7.2 0.7 all-gather.3.cloned.1.call-update
  7.9 3.4 %collective-permute-start = (bf16[1,256,2048]{2,1,0:T(8,128)(2,1)}, bf16[1,256,2048]{2,1,0:T(8,128)(2,1)S(1)}, u32[]{:S(2)}, u32[]{:S(2)}) collective-permute-start(bf16[1,256,2048]{2,1,0:T(8,128)(2,1)} %param.3), channel_id=1, source_target_pairs={{0,28},{4,0},{8,4},{12,8},{16,12},{20,16},{24,20},{28,24},{1,29},{... | collective-permute-start | bytes 3145736 | tf_op jit(solution)/shard_map/while/body/eval_jaxpr/ppermute | solution.py:9
  11.3 81.7 %all-gather.3.cloned.1.call-done = bf16[1,1024,2048]{2,1,0:T(8,128)(2,1)} async-done(((bf16[1,256,2048]{2,1,0:T(8,128)(2,1)}), bf16[1,1024,2048]{2,1,0:T(8,128)(2,1)}) %all-gather.3.cloned.1.call-update) | async-done | bytes 4194320 | tf_op jit(solution)/shard_map/all_gather | solution.py:23
  93.0 3.9 %fusion.7 = bf16[1024,256]{1,0:T(8,128)(2,1)S(1)} fusion(bf16[1,1024,2048]{2,1,0:T(8,128)(2,1)} %all-gather.3.cloned.1.call-done, bf16[1,256,2048]{2,1,0:T(8,128)(2,1)} %param.3), kind=kOutput, calls=%fused_computation.11 | convolution fusion | flops 1074003968 | bytes 5767168 | tf_op jit(solution)/shard_map/sjyp,ixp->isjyx/dot_general | solution.py:26
  97.0 1.4 fusion.10
  98.4 0.1 pad_maximum_fusion
  98.5 1.3 copy.10
  99.8 3.5 %all-to-all-start = ((bf16[1,2,1,256,4,256]{5,3,2,1,0,4:T(8,128)(2,1)}), bf16[1,2,1,256,4,256]{5,3,2,1,0,4:T(8,128)(2,1)S(1)}, u32[]{:S(2)}, u32[]{:S(2)}) async-start(bf16[1,2,1,256,4,256]{5,3,2,1,0,4:T(8,128)(2,1)} %copy.10), calls=%async_computation | async-start | bytes 2097152 | tf_op jit(solution)/shard_map/all_to_all | solution.py:41
  103.4 0.1 dynamic_slice.7
  103.5 0.6 dynamic_slice.6
  104.1 0.8 fusion.14
  104.9 0.1 broadcast_subtract_fusion
  105.0 24.2 %all-to-all-done = bf16[1,2,1,256,4,256]{5,3,2,1,0,4:T(8,128)(2,1)S(1)} async-done(((bf16[1,2,1,256,4,256]{5,3,2,1,0,4:T(8,128)(2,1)}), bf16[1,2,1,256,4,256]{5,3,2,1,0,4:T(8,128)(2,1)S(1)}, u32[]{:S(2)}, u32[]{:S(2)}) %all-to-all-start) | async-done | bytes 1048608 | tf_op jit(solution)/shard_map/all_to_all | solution.py:41
  129.2 1.9 fusion.5
  131.0 2.6 %bitcast_convert_fusion = bf16[1024,1024]{1,0:T(8,128)(2,1)} fusion(bf16[2,256,1024]{1,2,0:T(8,128)(2,1)S(1)} %bitcast.67, bf16[2,256,1024]{1,2,0:T(8,128)(2,1)S(1)} %bitcast.65), kind=kOutput, calls=%fused_computation | convolution fusion | flops 1074790400 | bytes 4194304 | tf_op jit(solution)/shard_map/dot_general | solution.py:68
  133.7 40.3 %reduce-scatter.3.cloned.1.call-done = bf16[128,1024]{1,0:T(8,128)(2,1)} async-done(((bf16[1024,1024]{1,0:T(8,128)(2,1)}), bf16[128,1024]{1,0:T(8,128)(2,1)}) %reduce-scatter.3.cloned.1.call-update) | async-done | bytes 262160 | tf_op jit(solution)/shard_map/reduce_scatter | solution.py:67
  174.0 1.8 convert_element_type.89
  175.8 1.1 copy.15
  176.9 1.1 copy.16
  178.1 3.0 %fusion.13 = f32[2,2]{1,0:T(2,128)S(1)} fusion(bf16[2,256,4,256]{3,0,2,1:T(2,128)(2,1)S(1)} %copy.15, bf16[2,256,4,256]{3,0,2,1:T(2,128)(2,1)S(1)} %copy.16), kind=kOutput, calls=%fused_computation.14 | convolution fusion | flops 2097156 | bytes 2097168 | tf_op jit(solution)/shard_map/dot_general | solution.py:78
  181.1 0.2 fusion.18
  181.3 0.3 fusion.17
  181.5 68.1 %all-gather = f32[256,8]{1,0:T(8,128)S(1)} all-gather(f32[8,8]{1,0:T(8,128)S(1)} %fusion.17), channel_id=2, replica_groups=mesh['occ'=8,'vir'=4] {'occ','vir'}, dimensions={0}, use_global_device_ids=true | all-gather | bytes 8448 | tf_op jit(solution)/shard_map/all_gather | solution.py:83
  249.6 0.6 bitcast_reduce_fusion
  (19 shorter events, 0.2 us)
Async XLA Ops:
  7.2 85.9 %all-gather.3.cloned.1.call-start = ((), (), s32[]{:S(2)}) async-start(), calls=%async_computation.3 | async-start | bytes 5242880 | tf_op jit(solution)/shard_map/all_gather | solution.py:23
  7.9 89.1 %collective-permute-start = (bf16[1,256,2048]{2,1,0:T(8,128)(2,1)}, bf16[1,256,2048]{2,1,0:T(8,128)(2,1)S(1)}, u32[]{:S(2)}, u32[]{:S(2)}) collective-permute-start(bf16[1,256,2048]{2,1,0:T(8,128)(2,1)} %param.3), channel_id=1, source_target_pairs={{0,28},{4,0},{8,4},{12,8},{16,12},{20,16},{24,20},{28,24},{1,29},{... | collective-permute-start | bytes 3145736 | tf_op jit(solution)/shard_map/while/body/eval_jaxpr/ppermute | solution.py:9
  93.0 4.0 %copy-start.3 = (bf16[1,1024,2048]{2,1,0:T(8,128)(2,1)S(1)}, bf16[1,1024,2048]{2,1,0:T(8,128)(2,1)}, u32[]{:S(2)}) copy-start(bf16[1,1024,2048]{2,1,0:T(8,128)(2,1)} %all-gather.3.cloned.1.call-done) | copy-start | bytes 12582916
  97.0 1.4 copy-start
  98.4 1.4 copy-start.1
  98.5 4.9 %copy-start.2 = (f32[1024]{0:T(1024)S(1)}, f32[1024]{0:T(1024)}, u32[]{:S(2)}) copy-start(f32[1024]{0:T(1024)} %param.5) | copy-start | bytes 12292
  98.5 5.0 %copy-start.4 = (f32[8]{0:T(128)S(1)}, f32[8]{0:T(128)}, u32[]{:S(2)}) copy-start(f32[8]{0:T(128)} %param.4) | copy-start | bytes 100
  99.8 29.4 %all-to-all-start = ((bf16[1,2,1,256,4,256]{5,3,2,1,0,4:T(8,128)(2,1)}), bf16[1,2,1,256,4,256]{5,3,2,1,0,4:T(8,128)(2,1)S(1)}, u32[]{:S(2)}, u32[]{:S(2)}) async-start(bf16[1,2,1,256,4,256]{5,3,2,1,0,4:T(8,128)(2,1)} %copy.10), calls=%async_computation | async-start | bytes 2097152 | tf_op jit(solution)/shard_map/all_to_all | solution.py:41
  103.3 70.7 %reduce-scatter.3.cloned.1.call-start = ((), (), s32[]{:S(2)}) async-start(), calls=%async_computation.4 | async-start | bytes 2359296 | tf_op jit(solution)/shard_map/reduce_scatter | solution.py:67
  133.7 116.6 %reduce-scatter.5.cloned.1.call-start = ((), (), s32[]{:S(2)}) async-start(), calls=%async_computation.5 | async-start | bytes 655360 | tf_op jit(solution)/shard_map/reduce_scatter | solution.py:75
Sparse Core Ops, SparseCore 0:
  9.5 83.4 all-gather.2
  133.8 40.1 reduce-scatter.2
  176.9 22.0 reduce-scatter.4
